TPU v7x, 32 devices: a whole 2x2x4 slice. The times are simulated.
32 devices in a mesh: pt: 8 (over z, y), tm: 4 (over x, core).
Axes of the slice: x: 2, y: 2, z: 4, core: 2. Of those that a mesh axis runs over, the one named last changes fastest.
Arguments:
- signals: float32 [512, 32768], P('pt', 'tm'), may hold values from -6 to 6
- freq_bins: int32 [4], replicated, may hold values from 1 to 511
Outputs:
- cross_spectra: float32 [2, 4, 512, 512], P(None, None, 'pt', 'tm')
All inputs are finite; a program needn't handle non-finite values.
Results may differ from a plain program's by a relative error of at most 0.000064.
Values sent between devices are 32-bit elements; how exact they have to be, the bound alone decides.
No kernel may reach another device: no remote copies, remote signals or barrier semaphores. Data moves between devices by JAX's collectives and lax.ppermute only.
A program may use at most 64 MiB of HBM per device.

v0:
```python
import math
import jax
import jax.numpy as jnp
from jax import lax
from jax.sharding import PartitionSpec as P

SEGLEN = 1024
TWO_PI = 2.0 * math.pi


def shifted(value, axis, steps):
    count = lax.axis_size(axis)
    initial, last = (max(0, -steps), min(count, count - steps))
    return lax.ppermute(value, axis, [(source, source + steps) for source in range(initial, last)])


def dft_tables(freq_bins, seg_len):
    sample_index = jnp.arange(seg_len, dtype=jnp.int32)
    wrapped = sample_index[:, None] * freq_bins[None, :] % seg_len
    angles = wrapped.astype(jnp.float32) * (TWO_PI / seg_len)
    window = 0.5 - 0.5 * jnp.cos(sample_index.astype(jnp.float32) * (TWO_PI / seg_len))
    cosine = window[:, None] * jnp.cos(angles)
    sine_part = -window[:, None] * jnp.sin(angles)
    full_table = jnp.concatenate([cosine, sine_part], axis=1)
    half_len = seg_len // 2
    return jnp.concatenate([full_table[:half_len], full_table[half_len:]], axis=1)


def tile_products(left_side, right_side):
    stacked_right = jnp.concatenate([right_side[:, 0], right_side[:, 1]], axis=2)
    real_left = jnp.concatenate([left_side[:, 0], left_side[:, 1]], axis=2)
    imag_left = jnp.concatenate([left_side[:, 1], -left_side[:, 0]], axis=2)
    real_part = jnp.einsum(
        "fps,fqs->fpq", real_left, stacked_right, precision=lax.Precision.HIGHEST
    )
    imag_part = jnp.einsum(
        "fps,fqs->fpq", imag_left, stacked_right, precision=lax.Precision.HIGHEST
    )
    return jnp.stack([real_part, imag_part])


def body(signals, freq_bins):
    point_rows, sample_count = signals.shape
    half_len = SEGLEN // 2
    blocks_dev = sample_count // half_len
    bin_count = freq_bins.shape[0]
    columns = 2 * bin_count
    table = dft_tables(freq_bins, SEGLEN)
    blocks = signals.reshape(point_rows, blocks_dev, half_len)
    projected = jnp.einsum("pbn,nc->pbc", blocks, table, precision=lax.Precision.HIGHEST)
    incoming = shifted(signals[:, :half_len], "tm", -1)
    boundary = jnp.dot(
        incoming,
        table[:, columns:],
        precision=lax.Precision.HIGHEST,
        preferred_element_type=jnp.float32,
    )
    following = jnp.concatenate([projected[:, 1:, columns:], boundary[:, None, :]], axis=1)
    spectra = projected[:, :, :columns] + following
    is_last = lax.axis_index("tm") == lax.axis_size("tm") - 1
    segment_ids = jnp.arange(blocks_dev, dtype=jnp.int32)
    weight_mask = jnp.where(
        jnp.logical_and(is_last, segment_ids == blocks_dev - 1), 0.0, 1.0
    ).astype(jnp.float32)
    spectra = spectra * weight_mask[None, :, None]
    spectra_panel = spectra.reshape(point_rows, blocks_dev, 2, bin_count).transpose(3, 2, 0, 1)
    partial_tiles = tile_products(
        spectra_panel, lax.all_gather(spectra_panel, "pt", axis=2, tiled=True)
    )
    summed = lax.psum_scatter(partial_tiles, "tm", scatter_dimension=3, tiled=True)
    total_segments = blocks_dev * lax.axis_size("tm") - 1
    scale = 1.0 / (total_segments * 0.375 * SEGLEN)
    return summed * scale


def solution(mesh):
    in_specs = (P("pt", "tm"), P())
    out_specs = P(None, None, "pt", "tm")
    return jax.shard_map(body, mesh=mesh, in_specs=in_specs, out_specs=out_specs, check_vma=False)
```

profile of v0, /device:TPU:0, one launch (start us, length us, event | category | flops | bytes accessed | tf_op | source)
XLA Modules:
  0.0 97.8 jit_solution(1529557021851676892)
XLA Ops:
  6.5 0.0 reduce-scatter.2.cloned.1.call-start
  6.5 0.9 slice.33
  7.5 1.3 %collective-permute-start = (f32[64,512]{1,0:T(8,128)S(1)}, f32[64,512]{1,0:T(8,128)S(1)}, u32[]{:S(2)}, u32[]{:S(2)}) collective-permute-start(f32[64,512]{1,0:T(8,128)S(1)} %slice.33), channel_id=1, source_target_pairs={{1,0},{2,1},{3,2},{5,4},{6,5},{7,6},{9,8},{10,9},{11,10},{13,12},{... | collective-permute-start | bytes 393224 | tf_op jit(solution)/shard_map/ppermute | solution.py:14
  8.8 0.9 cosine_multiply_fusion
  9.7 4.2 %fusion.3 = f32[64,16,16]{0,2,1:T(8,128)S(1)} fusion(f32[8,16,8,512]{3,2,1,0:T(8,128)} %bitcast.33, f32[512,8]{0,1:T(8,128)S(1)} %get-tuple-element.10, f32[512,8]{0,1:T(8,128)S(1)} %get-tuple-element.9), kind=kOutput, calls=%fused_computation.5 | convolution fusion | flops 100671488 | bytes 2195456 | tf_op jit(solution)/shard_map/pbn,nc->pbc/dot_general | solution.py:50
  13.9 0.0 collective-permute-done
  13.9 0.2 convolution_bitcast_fusion.2
  14.1 0.1 fusion.6
  14.2 0.2 copy.7
  14.4 47.1 %all_gather.3 = f32[4,2,512,16]{3,0,1,2:T(4,128)S(1)} all-gather(f32[4,2,64,16]{3,0,1,2:T(4,128)S(1)} %copy.7), channel_id=1, replica_groups=mesh['pt'=8,'tm'=4] {'pt'}, dimensions={2}, use_global_device_ids=true | all-gather | bytes 294912 | tf_op jit(solution)/shard_map/all_gather | solution.py:68
  61.5 0.4 fusion.24
  61.9 0.3 copy.10
  62.2 0.3 copy.11
  62.5 0.6 convolution_bitcast_fusion.1
  63.2 0.6 convolution_bitcast_fusion
  63.8 1.0 %pad_maximum_fusion = f32[2,4,64,512]{3,2,1,0:T(8,128)} fusion(f32[1,4,64,512]{3,2,1,0:T(8,128)S(1)} %convolution_bitcast_fusion, f32[1,4,64,512]{3,2,1,0:T(8,128)S(1)} %convolution_bitcast_fusion.1), kind=kLoop, calls=%fused_computation.7 | loop fusion | flops 262144 | bytes 2097152 | tf_op jit(solution)/shard_map/stack | solution.py:39
  64.9 0.0 reduce-scatter.2.cloned.1.call-update
  64.9 24.3 %reduce-scatter.2.cloned.1.call-done = f32[2,4,64,128]{3,2,1,0:T(8,128)} async-done(((f32[2,4,64,512]{3,2,1,0:T(8,128)}), f32[2,4,64,128]{3,2,1,0:T(8,128)}) %reduce-scatter.2.cloned.1.call-update) | async-done | bytes 262160 | tf_op jit(solution)/shard_map/reduce_scatter | solution.py:70
  89.2 1.7 %broadcast_multiply_fusion = f32[2,4,64,128]{3,2,1,0:T(8,128)} fusion(f32[2,4,64,128]{3,2,1,0:T(8,128)} %reduce-scatter.2.cloned.1.call-done), kind=kLoop, calls=%fused_computation.9 | loop fusion | flops 65536 | bytes 524288 | tf_op jit(solution)/shard_map/mul | solution.py:73
  (7 shorter events, 0.1 us)
Async XLA Ops:
  6.5 82.7 %reduce-scatter.2.cloned.1.call-start = ((), (), s32[]{:S(2)}) async-start(), calls=%async_computation.1 | async-start | bytes 1310720 | tf_op jit(solution)/shard_map/reduce_scatter | solution.py:70
  7.5 6.4 %collective-permute-start = (f32[64,512]{1,0:T(8,128)S(1)}, f32[64,512]{1,0:T(8,128)S(1)}, u32[]{:S(2)}, u32[]{:S(2)}) collective-permute-start(f32[64,512]{1,0:T(8,128)S(1)} %slice.33), channel_id=1, source_target_pairs={{1,0},{2,1},{3,2},{5,4},{6,5},{7,6},{9,8},{10,9},{11,10},{13,12},{... | collective-permute-start | bytes 393224 | tf_op jit(solution)/shard_map/ppermute | solution.py:14
Sparse Core Ops, SparseCore 0:
  65.0 24.1 reduce-scatter.1
where the time goes:
time: 98 us; the launch traced here: 97.8 us
  blocking collectives  47.1 us (48%)
  waiting for transfers between devices  24.4 us (25%)
  between operations  13.5 us (14%)
  matrix products  5.6 us (6%)
  other arithmetic  3.79 us (4%)
  local copies, waits for them, and re-layouts  2.13 us (2%)
  starting transfers between devices  1.29 us (1%)
    all_gather x1, blocking collectives, body(): lax.all_gather(spectra_panel, 'pt', axis=2, tiled=True)  47.1 us
    reduce_scatter x1, waiting for transfers between devices, body(): lax.psum_scatter(partial_tiles, 'tm', scatter_dimension=3, tiled=True)  24.3 us
    dot_general x1, matrix products, body(): jnp.einsum('pbn,nc->pbc', blocks, table, precision=lax.Precision.HIGHEST)  4.15 us
  transfers between devices with their start and end apart: 2, of which 1 were waited for; matrix products, arithmetic and copies ran while one was open for 5% of the time, Pallas kernels for 0%

commit v1 on v0

--- a/solution.py
+++ b/solution.py
@@ -6,6 +6,19 @@
 
 SEGLEN = 1024
 TWO_PI = 2.0 * math.pi
+
+
+def ring_gather(array, axis, dim):
+    ways = lax.axis_size(axis)
+    up = [(d, (d + 1) % ways) for d in range(ways)]
+    down = [(d, (d - 1) % ways) for d in range(ways)]
+    earlier, later = ([array], [array])
+    for _ in range(ways // 2):
+        earlier.append(lax.ppermute(earlier[-1], axis, up))
+    for _ in range((ways - 1) // 2):
+        later.append(lax.ppermute(later[-1], axis, down))
+    line = jnp.concatenate([*earlier[::-1], *later[1:]], axis=dim)
+    return jnp.roll(line, (lax.axis_index(axis) - ways // 2) * array.shape[dim], axis=dim)
 
 
 def shifted(value, axis, steps):
@@ -64,9 +77,7 @@
     ).astype(jnp.float32)
     spectra = spectra * weight_mask[None, :, None]
     spectra_panel = spectra.reshape(point_rows, blocks_dev, 2, bin_count).transpose(3, 2, 0, 1)
-    partial_tiles = tile_products(
-        spectra_panel, lax.all_gather(spectra_panel, "pt", axis=2, tiled=True)
-    )
+    partial_tiles = tile_products(spectra_panel, ring_gather(spectra_panel, "pt", 2))
     summed = lax.psum_scatter(partial_tiles, "tm", scatter_dimension=3, tiled=True)
     total_segments = blocks_dev * lax.axis_size("tm") - 1
     scale = 1.0 / (total_segments * 0.375 * SEGLEN)

time: 98 us -> 78.4 us (0.80)
  blocking collectives: 47.1 us -> 0 us
  starting transfers between devices: 1.29 us -> 16.7 us
  waiting for transfers between devices: 24.4 us -> 37.2 us
    all_gather x1 -> x0, blocking collectives: 47.1 us -> none  [body(): lax.all_gather(spectra_panel, 'pt', axis=2, tiled=True)]
    ppermute x0 -> x7, starting transfers between devices: none -> 15.4 us  [the longest x3 12.4 us: ring_gather(): later.append(lax.ppermute(later[-1], axis, down))]
    ppermute x0 -> x7, waiting for transfers between devices: none -> 14.2 us  [the longest x4 13.7 us: ring_gather(): earlier.append(lax.ppermute(earlier[-1], axis, up))]
    reduce_scatter x1, waiting for transfers between devices: 24.3 us -> 23 us  [body(): lax.psum_scatter(partial_tiles, 'tm', scatter_dimension=3, tiled=True)]
  transfers between devices with their start and end apart: 2 -> 9, of which waited for: 1 -> 6; matrix products, arithmetic and copies ran while one was open for 5% -> 7% of each run, Pallas kernels for 0% -> 0%
where the time goes in v1:
time: 78.4 us; the launch traced here: 78.2 us
  waiting for transfers between devices  37.2 us (47%)
  starting transfers between devices  16.7 us (21%)
  between operations  13.5 us (17%)
  matrix products  5.59 us (7%)
  other arithmetic  3.79 us (5%)
  local copies, waits for them, and re-layouts  1.36 us (2%)
    reduce_scatter x1, waiting for transfers between devices, body(): lax.psum_scatter(partial_tiles, 'tm', scatter_dimension=3, tiled=True)  23 us
    ppermute x4, waiting for transfers between devices, ring_gather(): earlier.append(lax.ppermute(earlier[-1], axis, up))  13.7 us
    ppermute x3, starting transfers between devices, ring_gather(): later.append(lax.ppermute(later[-1], axis, down))  12.4 us
    dot_general x1, matrix products, body(): jnp.einsum('pbn,nc->pbc', blocks, table, precision=lax.Precision.HIGHEST)  4.15 us
    ppermute x4, starting transfers between devices, ring_gather(): earlier.append(lax.ppermute(earlier[-1], axis, up))  3.03 us
    mul x1, other arithmetic, body(): return summed * scale  1.68 us
  transfers between devices with their start and end apart: 9, of which 6 were waited for; matrix products, arithmetic and copies ran while one was open for 7% of the time, Pallas kernels for 0%

profile of v1, /device:TPU:0, one launch (start us, length us, event | category | flops | bytes accessed | tf_op | source)
XLA Modules:
  0.0 78.2 jit_solution(13676473897289106559)
XLA Ops:
  6.5 0.0 reduce-scatter.2.cloned.1.call-start
  6.5 0.9 %slice.33 = f32[64,512]{1,0:T(8,128)S(1)} slice(f32[64,8192]{1,0:T(8,128)} %param.2), slice={[0:64], [0:512]} | slice | bytes 262144 | tf_op jit(solution)/shard_map/slice | solution.py:64
  7.5 1.3 %collective-permute-start = (f32[64,512]{1,0:T(8,128)S(1)}, f32[64,512]{1,0:T(8,128)S(1)}, u32[]{:S(2)}, u32[]{:S(2)}) collective-permute-start(f32[64,512]{1,0:T(8,128)S(1)} %slice.33), channel_id=1, source_target_pairs={{1,0},{2,1},{3,2},{5,4},{6,5},{7,6},{9,8},{10,9},{11,10},{13,12},{... | collective-permute-start | bytes 393224 | tf_op jit(solution)/shard_map/ppermute | solution.py:27
  8.8 0.9 %cosine_multiply_fusion = (f32[1024,4]{0,1:T(4,128)S(1)}, f32[1024,4]{0,1:T(4,128)S(1)}) fusion(s32[4]{0:T(128)} %param.3, f32[1024]{0:T(1024)S(1)} %get-tuple-element.13, f32[1024]{0:T(1024)S(1)} %get-tuple-element.14), kind=kLoop, calls=%fused_computation.37 | loop fusion | flops 65536 | bytes 40976 | tf_op jit(solution)/shard_map/mul | solution.py:35
  9.7 4.2 %fusion.3 = f32[64,16,16]{0,2,1:T(8,128)S(1)} fusion(f32[8,16,8,512]{3,2,1,0:T(8,128)} %bitcast.35, f32[512,8]{0,1:T(8,128)S(1)} %get-tuple-element.10, f32[512,8]{0,1:T(8,128)S(1)} %get-tuple-element.9), kind=kOutput, calls=%fused_computation.5 | convolution fusion | flops 100671488 | bytes 2195456 | tf_op jit(solution)/shard_map/pbn,nc->pbc/dot_general | solution.py:63
  13.9 0.0 collective-permute-done
  13.9 0.2 convolution_bitcast_fusion.2
  14.1 0.1 fusion.6
  14.2 3.0 %collective-permute-start.1 = (f32[4,2,64,16]{2,3,0,1:T(8,128)S(1)}, f32[4,2,64,16]{2,3,0,1:T(8,128)S(1)}, u32[]{:S(2)}, u32[]{:S(2)}) collective-permute-start(f32[4,2,64,16]{2,3,0,1:T(8,128)S(1)} %bitcast.36), channel_id=1, source_target_pairs={{0,4},{4,8},{8,12},{12,16},{16,20},{20,24},{24,28},{28,0},{1,5},{5... | collective-permute-start | bytes 98312 | tf_op jit(solution)/shard_map/ppermute | solution.py:17
  17.3 3.1 %collective-permute-start.5 = (f32[4,2,64,16]{2,3,0,1:T(8,128)S(1)}, f32[4,2,64,16]{2,3,0,1:T(8,128)S(1)}, u32[]{:S(2)}, u32[]{:S(2)}) collective-permute-start(f32[4,2,64,16]{2,3,0,1:T(8,128)S(1)} %bitcast.37), channel_id=1, source_target_pairs={{0,28},{4,0},{8,4},{12,8},{16,12},{20,16},{24,20},{28,24},{1,29},{... | collective-permute-start | bytes 98312 | tf_op jit(solution)/shard_map/ppermute | solution.py:19
  20.4 2.6 %collective-permute-done.1 = f32[4,2,64,16]{2,3,0,1:T(8,128)S(1)} collective-permute-done((f32[4,2,64,16]{2,3,0,1:T(8,128)S(1)}, f32[4,2,64,16]{2,3,0,1:T(8,128)S(1)}, u32[]{:S(2)}, u32[]{:S(2)}) %collective-permute-start.1) | collective-permute-done | bytes 32800 | tf_op jit(solution)/shard_map/ppermute | solution.py:17
  23.0 0.0 collective-permute-start.2
  23.0 0.5 collective-permute-done.5
  23.5 4.4 %collective-permute-start.6 = (f32[4,2,64,16]{2,3,0,1:T(8,128)S(1)}, f32[4,2,64,16]{2,3,0,1:T(8,128)S(1)}, u32[]{:S(2)}, u32[]{:S(2)}) collective-permute-start(f32[4,2,64,16]{2,3,0,1:T(8,128)S(1)} %collective-permute-done.5), channel_id=1, source_target_pairs={{0,28},{4,0},{8,4},{12,8},{16,12},{20,16},{24,20},{28,24},{1,29},{... | collective-permute-start | bytes 98312 | tf_op jit(solution)/shard_map/ppermute | solution.py:19
  27.9 2.1 %collective-permute-done.2 = f32[4,2,64,16]{2,3,0,1:T(8,128)S(1)} collective-permute-done((f32[4,2,64,16]{2,3,0,1:T(8,128)S(1)}, f32[4,2,64,16]{2,3,0,1:T(8,128)S(1)}, u32[]{:S(2)}, u32[]{:S(2)}) %collective-permute-start.2) | collective-permute-done | bytes 32800 | tf_op jit(solution)/shard_map/ppermute | solution.py:17
  29.9 0.0 collective-permute-start.3
  30.0 0.0 collective-permute-done.6
  30.0 4.9 %collective-permute-start.7 = (f32[4,2,64,16]{2,3,0,1:T(8,128)S(1)}, f32[4,2,64,16]{2,3,0,1:T(8,128)S(1)}, u32[]{:S(2)}, u32[]{:S(2)}) collective-permute-start(f32[4,2,64,16]{2,3,0,1:T(8,128)S(1)} %collective-permute-done.6), channel_id=1, source_target_pairs={{0,28},{4,0},{8,4},{12,8},{16,12},{20,16},{24,20},{28,24},{1,29},{... | collective-permute-start | bytes 98312 | tf_op jit(solution)/shard_map/ppermute | solution.py:19
  34.9 2.0 %collective-permute-done.3 = f32[4,2,64,16]{2,3,0,1:T(8,128)S(1)} collective-permute-done((f32[4,2,64,16]{2,3,0,1:T(8,128)S(1)}, f32[4,2,64,16]{2,3,0,1:T(8,128)S(1)}, u32[]{:S(2)}, u32[]{:S(2)}) %collective-permute-start.3) | collective-permute-done | bytes 32800 | tf_op jit(solution)/shard_map/ppermute | solution.py:17
  36.9 0.0 collective-permute-start.4
  36.9 0.0 collective-permute-done.7
  36.9 6.9 %collective-permute-done.4 = f32[4,2,64,16]{2,3,0,1:T(8,128)S(1)} collective-permute-done((f32[4,2,64,16]{2,3,0,1:T(8,128)S(1)}, f32[4,2,64,16]{2,3,0,1:T(8,128)S(1)}, u32[]{:S(2)}, u32[]{:S(2)}) %collective-permute-start.4) | collective-permute-done | bytes 32800 | tf_op jit(solution)/shard_map/ppermute | solution.py:17
  43.9 0.3 concatenate.28
  44.2 0.1 dynamic-slice_bitcast_fusion.1
  44.3 0.6 convolution_bitcast_fusion
  44.9 0.6 convolution_bitcast_fusion.1
  45.6 1.0 %pad_maximum_fusion = f32[2,4,64,512]{3,2,1,0:T(8,128)} fusion(f32[1,4,64,512]{3,2,1,0:T(8,128)S(1)} %convolution_bitcast_fusion, f32[1,4,64,512]{3,2,1,0:T(8,128)S(1)} %convolution_bitcast_fusion.1), kind=kLoop, calls=%fused_computation.7 | loop fusion | flops 262144 | bytes 2097152 | tf_op jit(solution)/shard_map/stack | solution.py:52
  46.6 0.0 reduce-scatter.2.cloned.1.call-update
  46.6 23.0 %reduce-scatter.2.cloned.1.call-done = f32[2,4,64,128]{3,2,1,0:T(8,128)} async-done(((f32[2,4,64,512]{3,2,1,0:T(8,128)}), f32[2,4,64,128]{3,2,1,0:T(8,128)}) %reduce-scatter.2.cloned.1.call-update) | async-done | bytes 262160 | tf_op jit(solution)/shard_map/reduce_scatter | solution.py:81
  69.6 1.7 %broadcast_multiply_fusion = f32[2,4,64,128]{3,2,1,0:T(8,128)} fusion(f32[2,4,64,128]{3,2,1,0:T(8,128)} %reduce-scatter.2.cloned.1.call-done), kind=kLoop, calls=%fused_computation.11 | loop fusion | flops 65536 | bytes 524288 | tf_op jit(solution)/shard_map/mul | solution.py:84
  (7 shorter events, 0.1 us)
Async XLA Ops:
  6.5 63.1 %reduce-scatter.2.cloned.1.call-start = ((), (), s32[]{:S(2)}) async-start(), calls=%async_computation.1 | async-start | bytes 1310720 | tf_op jit(solution)/shard_map/reduce_scatter | solution.py:81
  7.5 6.4 %collective-permute-start = (f32[64,512]{1,0:T(8,128)S(1)}, f32[64,512]{1,0:T(8,128)S(1)}, u32[]{:S(2)}, u32[]{:S(2)}) collective-permute-start(f32[64,512]{1,0:T(8,128)S(1)} %slice.33), channel_id=1, source_target_pairs={{1,0},{2,1},{3,2},{5,4},{6,5},{7,6},{9,8},{10,9},{11,10},{13,12},{... | collective-permute-start | bytes 393224 | tf_op jit(solution)/shard_map/ppermute | solution.py:27
  14.2 8.7 %collective-permute-start.1 = (f32[4,2,64,16]{2,3,0,1:T(8,128)S(1)}, f32[4,2,64,16]{2,3,0,1:T(8,128)S(1)}, u32[]{:S(2)}, u32[]{:S(2)}) collective-permute-start(f32[4,2,64,16]{2,3,0,1:T(8,128)S(1)} %bitcast.36), channel_id=1, source_target_pairs={{0,4},{4,8},{8,12},{12,16},{16,20},{20,24},{24,28},{28,0},{1,5},{5... | collective-permute-start | bytes 98312 | tf_op jit(solution)/shard_map/ppermute | solution.py:17
  17.3 6.2 %collective-permute-start.5 = (f32[4,2,64,16]{2,3,0,1:T(8,128)S(1)}, f32[4,2,64,16]{2,3,0,1:T(8,128)S(1)}, u32[]{:S(2)}, u32[]{:S(2)}) collective-permute-start(f32[4,2,64,16]{2,3,0,1:T(8,128)S(1)} %bitcast.37), channel_id=1, source_target_pairs={{0,28},{4,0},{8,4},{12,8},{16,12},{20,16},{24,20},{28,24},{1,29},{... | collective-permute-start | bytes 98312 | tf_op jit(solution)/shard_map/ppermute | solution.py:19
  23.0 7.0 %collective-permute-start.2 = (f32[4,2,64,16]{2,3,0,1:T(8,128)S(1)}, f32[4,2,64,16]{2,3,0,1:T(8,128)S(1)}, u32[]{:S(2)}, u32[]{:S(2)}) collective-permute-start(f32[4,2,64,16]{2,3,0,1:T(8,128)S(1)} %collective-permute-done.1), channel_id=1, source_target_pairs={{0,4},{4,8},{8,12},{12,16},{16,20},{20,24},{24,28},{28,0},{1,5},{5... | collective-permute-start | bytes 98312 | tf_op jit(solution)/shard_map/ppermute | solution.py:17
  23.5 6.5 %collective-permute-start.6 = (f32[4,2,64,16]{2,3,0,1:T(8,128)S(1)}, f32[4,2,64,16]{2,3,0,1:T(8,128)S(1)}, u32[]{:S(2)}, u32[]{:S(2)}) collective-permute-start(f32[4,2,64,16]{2,3,0,1:T(8,128)S(1)} %collective-permute-done.5), channel_id=1, source_target_pairs={{0,28},{4,0},{8,4},{12,8},{16,12},{20,16},{24,20},{28,24},{1,29},{... | collective-permute-start | bytes 98312 | tf_op jit(solution)/shard_map/ppermute | solution.py:19
  29.9 7.0 %collective-permute-start.3 = (f32[4,2,64,16]{2,3,0,1:T(8,128)S(1)}, f32[4,2,64,16]{2,3,0,1:T(8,128)S(1)}, u32[]{:S(2)}, u32[]{:S(2)}) collective-permute-start(f32[4,2,64,16]{2,3,0,1:T(8,128)S(1)} %collective-permute-done.2), channel_id=1, source_target_pairs={{0,4},{4,8},{8,12},{12,16},{16,20},{20,24},{24,28},{28,0},{1,5},{5... | collective-permute-start | bytes 98312 | tf_op jit(solution)/shard_map/ppermute | solution.py:17
  30.0 7.0 %collective-permute-start.7 = (f32[4,2,64,16]{2,3,0,1:T(8,128)S(1)}, f32[4,2,64,16]{2,3,0,1:T(8,128)S(1)}, u32[]{:S(2)}, u32[]{:S(2)}) collective-permute-start(f32[4,2,64,16]{2,3,0,1:T(8,128)S(1)} %collective-permute-done.6), channel_id=1, source_target_pairs={{0,28},{4,0},{8,4},{12,8},{16,12},{20,16},{24,20},{28,24},{1,29},{... | collective-permute-start | bytes 98312 | tf_op jit(solution)/shard_map/ppermute | solution.py:19
  36.9 7.0 %collective-permute-start.4 = (f32[4,2,64,16]{2,3,0,1:T(8,128)S(1)}, f32[4,2,64,16]{2,3,0,1:T(8,128)S(1)}, u32[]{:S(2)}, u32[]{:S(2)}) collective-permute-start(f32[4,2,64,16]{2,3,0,1:T(8,128)S(1)} %collective-permute-done.3), channel_id=1, source_target_pairs={{0,4},{4,8},{8,12},{12,16},{16,20},{20,24},{24,28},{28,0},{1,5},{5... | collective-permute-start | bytes 98312 | tf_op jit(solution)/shard_map/ppermute | solution.py:17
Sparse Core Ops, SparseCore 0:
  46.8 22.8 reduce-scatter.1
